TPU v7x, 256 devices: a whole 4x4x8 slice. The times are simulated.
256 devices in a mesh: curve: 32 (over y_hi, z, core), tm: 8 (over y_lo, x).
Axes of the slice: x: 4, y: 4 (y_hi: 2, y_lo: 2; y = y_hi * 2 + y_lo), z: 8, core: 2. Of those that a mesh axis runs over, the one named last changes fastest.
Arguments:
- samples: float32 [8192, 65536], P('curve', 'tm'), may hold values from -30 to 30
- smoothing: float32 [8192], P('curve'), may hold values from 0.5 to 20
- test_matrix: float32 [4096, 64], P('tm'), may hold values from -0.75 to 0.75
- sketch_prev: float32 [4096, 64], P('tm', 'curve'), may hold values from -1.2 to 1.2
Outputs:
- coefficients: float32 [8192, 4096], P('curve', 'tm')
- scores: float32 [8192, 64], P('curve')
- sketch: float32 [4096, 64], P('tm', 'curve')
All inputs are finite; a program needn't handle non-finite values.
Results may differ from a plain program's by a relative error of at most 0.0002.
Values sent between devices are 32-bit elements; how exact they have to be, the bound alone decides.
A program may use at most 64 MiB of HBM per device.

v0:
```python
import jax
import jax.numpy as jnp
from jax import lax
from jax.sharding import PartitionSpec as P

SPB = 16
ITERS = 4


damping = 0.45


def passed_along(block, axis, distance):
    devices = range(lax.axis_size(axis))
    route = [(i - distance, i) for i in devices if i - distance in devices]
    return lax.ppermute(block, axis, route)


def padded_2(block, sides, width):
    for axis, dim in sides:
        count = lax.axis_size(axis)
        forward = [(i, i + 1) for i in range(count - 1)]
        backward = [(target, source) for source, target in forward]
        low = lax.ppermute(
            lax.slice_in_dim(block, block.shape[dim] - width, None, axis=dim), axis, forward
        )
        high = lax.ppermute(lax.slice_in_dim(block, 0, width, axis=dim), axis, backward)
        block = jnp.concatenate([low, block, high], axis=dim)
    return block


def sent_to_all(value, axis):
    copies = jnp.broadcast_to(value, (lax.axis_size(axis), *value.shape))
    return lax.all_to_all(copies, axis, split_axis=0, concat_axis=0, tiled=True)


def of_everyone(value, axis):
    return sent_to_all(value, axis).sum(axis=0)


def cut_along(value, dim, devices):
    before, after = (value.shape[:dim], value.shape[dim + 1 :])
    return jnp.moveaxis(value.reshape(*before, devices, -1, *after), dim, 0)


def sent_and_summed(value, axis, dim):
    pieces = cut_along(value, dim, lax.axis_size(axis))
    arrived = lax.all_to_all(pieces, axis, split_axis=0, concat_axis=0, tiled=True)
    return arrived.sum(axis=0)


def weight_table():
    frac = (jnp.arange(SPB, dtype=jnp.float32) + 0.5) / SPB
    pieces = [
        frac**3 / 6.0,
        (-3.0 * frac**3 + 3.0 * frac**2 + 3.0 * frac + 1.0) / 6.0,
        (3.0 * frac**3 - 6.0 * frac**2 + 4.0) / 6.0,
        (1.0 - frac) ** 3 / 6.0,
    ]
    return jnp.stack(pieces) / SPB


def relax_sweep(widened, target, smooth_col, index_wide, total_basis):
    second = widened[:, 2:] - 2.0 * widened[:, 1:-1] + widened[:, :-2]
    in_range = (index_wide[:-2] >= 0) & (index_wide[:-2] <= total_basis - 3)
    second = jnp.where(in_range[None, :], second, 0.0)
    bending = second[:, 2:] - 2.0 * second[:, 1:-1] + second[:, :-2]
    interior = widened[:, 2:-2]
    column_index = index_wide[2:-2]
    penalty_diag = (
        (column_index <= total_basis - 3).astype(jnp.float32)
        + 4.0 * ((column_index >= 1) & (column_index <= total_basis - 2)).astype(jnp.float32)
        + (column_index >= 2).astype(jnp.float32)
    )
    return interior + damping * (target - interior - smooth_col * bending) / (
        1.0 + smooth_col * penalty_diag
    )


def body(samples, smoothing, test_matrix, sketch_prev):
    row_count = samples.shape[0]
    basis_width = samples.shape[1] // SPB
    blocks = samples.reshape(row_count, basis_width, SPB)
    segment_sums = jnp.einsum(
        "cgq,mq->mcg", blocks, weight_table(), precision=lax.Precision.HIGHEST
    )
    padded = jnp.pad(segment_sums, ((0, 0), (0, 0), (3, 3)))
    extended = (
        padded[0, :, 0 : basis_width + 3]
        + padded[1, :, 1 : basis_width + 4]
        + padded[2, :, 2 : basis_width + 5]
        + padded[3, :, 3 : basis_width + 6]
    )
    spilled = extended[:, basis_width:]
    arrived = passed_along(spilled, "tm", 1)
    proj = jnp.concatenate([extended[:, :3] + arrived, extended[:, 3:basis_width]], axis=1)
    total_basis = basis_width * lax.axis_size("tm")
    first_column = lax.axis_index("tm") * basis_width
    smooth_col = smoothing[:, None]
    margin = 2 * ITERS
    proj_wide = padded_2(proj, (("tm", 1),), margin)
    coefficients = proj_wide
    for sweep_number in range(ITERS):
        margin_now = margin - 2 * sweep_number
        index_wide = (
            first_column - margin_now + jnp.arange(basis_width + 2 * margin_now, dtype=jnp.int32)
        )
        offset = 2 * sweep_number + 2
        target = proj_wide[:, offset : offset + basis_width + 2 * margin_now - 4]
        coefficients = relax_sweep(coefficients, target, smooth_col, index_wide, total_basis)
    curve_total = row_count * lax.axis_size("curve")
    totals = of_everyone(jnp.sum(coefficients, axis=0), "curve")
    column_mean = totals / curve_total
    centered = coefficients - column_mean[None, :]
    partial_value = jnp.dot(
        centered, test_matrix, precision=lax.Precision.HIGHEST, preferred_element_type=jnp.float32
    )
    scores = of_everyone(partial_value, "tm")
    sketch_part = (
        jnp.einsum("ck,cr->kr", centered, scores, precision=lax.Precision.HIGHEST) / curve_total
    )
    owned_part = sent_and_summed(sketch_part, "curve", 1)
    return (coefficients, scores, sketch_prev + owned_part)


def solution(mesh):
    placed = (P("curve", "tm"), P("curve"), P("tm", None), P("tm", "curve"))
    return jax.shard_map(
        body,
        mesh=mesh,
        in_specs=placed,
        out_specs=(P("curve", "tm"), P("curve", None), P("tm", "curve")),
        check_vma=False,
    )
```

profile of v0, /device:TPU:1, one launch (start us, length us, event | category | flops | bytes accessed | tf_op | source)
XLA Modules:
  0.0 102.3 jit_solution(1103452611978341890)
XLA Ops:
  0.6 0.0 copy-start
  0.7 9.0 %copy.22 = f32[256,8192]{0,1:T(8,128)} copy(f32[256,8192]{1,0:T(8,128)} %param.4) | data formatting | bytes 16777216 | tf_op args[0]
  9.7 10.5 %copy.23 = f32[256,512,16]{1,2,0:T(8,128)} copy(f32[256,512,16]{0,2,1:T(8,128)} %bitcast.11) | data formatting | bytes 16777216 | tf_op jit(solution)/shard_map/reshape | solution.py:83
  20.2 0.0 copy-start.2
  20.2 6.4 %fusion.43 = f32[4,256,512]{2,0,1:T(4,128)S(1)} fusion(f32[256,512,16]{1,2,0:T(8,128)} %copy.23, f32[1,16]{1,0:T(1,128)S(1)} %get-tuple-element.17, f32[1,16]{1,0:T(1,128)S(1)} %get-tuple-element.18, f32[1,16]{1,0:T(1,128)S(1)} %get-tuple-element.19, f32[1,16]{1,0:T(1,128)S(1)} %get-tuple-element.20), kind=kOutput, calls=%fused_computation.83 | convolution fusion | flops 100663552 | bytes 10486016 | tf_op jit(solution)/shard_map/cgq,mq->mcg/dot_general | solution.py:84
  26.6 4.7 %fusion.2 = f32[1,256,515]{2,0,1:T(1,128)S(1)} fusion(f32[4,256,512]{2,0,1:T(4,128)S(1)} %fusion.43), kind=kLoop, calls=%fused_computation.9 | loop fusion | flops 395520 | bytes 2624512 | tf_op jit(solution)/shard_map/add | solution.py:89
  31.3 0.4 copy.24
  31.7 3.9 %collective-permute-start.1 = (f32[256,3]{0,1:T(4,128)S(1)}, f32[256,3]{0,1:T(4,128)S(1)}, u32[]{:S(2)}, u32[]{:S(2)}) collective-permute-start(f32[256,3]{0,1:T(4,128)S(1)} %slice.196), channel_id=1, source_target_pairs={{0,1},{1,2},{2,3},{3,4},{4,5},{5,6},{6,7},{8,9},{9,10},{10,11},{11... | collective-permute-start | bytes 9224 | tf_op jit(solution)/shard_map/ppermute | solution.py:16
  35.7 3.1 %collective-permute-start = (f32[256,8]{0,1:T(8,128)S(1)}, f32[256,8]{0,1:T(8,128)S(1)}, u32[]{:S(2)}, u32[]{:S(2)}) collective-permute-start(f32[256,8]{0,1:T(8,128)S(1)} %slice.194), channel_id=1, source_target_pairs={{0,1},{1,2},{2,3},{3,4},{4,5},{5,6},{6,7},{8,9},{9,10},{10,11},{11... | collective-permute-start | bytes 24584 | tf_op jit(solution)/shard_map/ppermute | solution.py:24
  38.9 0.1 convert_add_fusion.2
  38.9 0.1 convert_add_fusion.1
  39.0 0.1 convert_add_fusion
  39.1 0.1 convert_add_fusion.3
  39.2 0.0 collective-permute-done.1
  39.3 1.3 %collective-permute-start.2 = (f32[256,8]{0,1:T(8,128)S(1)}, f32[256,8]{0,1:T(8,128)S(1)}, u32[]{:S(2)}, u32[]{:S(2)}) collective-permute-start(f32[256,8]{0,1:T(8,128)S(1)} %fusion.41), channel_id=1, source_target_pairs={{1,0},{2,1},{3,2},{4,3},{5,4},{6,5},{7,6},{9,8},{10,9},{11,10},{12... | collective-permute-start | bytes 24584 | tf_op jit(solution)/shard_map/ppermute | solution.py:27
  40.6 0.0 collective-permute-done
  40.6 3.1 %collective-permute-done.2 = f32[256,8]{0,1:T(8,128)S(1)} collective-permute-done((f32[256,8]{0,1:T(8,128)S(1)}, f32[256,8]{0,1:T(8,128)S(1)}, u32[]{:S(2)}, u32[]{:S(2)}) %collective-permute-start.2) | collective-permute-done | bytes 8224 | tf_op jit(solution)/shard_map/ppermute | solution.py:27
  43.7 0.2 fusion.11
  43.9 0.0 copy-done.2
  43.9 0.3 fusion.9
  44.2 0.2 fusion.3
  44.4 0.4 fusion.27
  44.7 0.0 copy-start.3
  44.8 0.2 fusion.21
  44.9 0.4 fusion.19
  45.3 0.2 fusion.13
  45.4 0.5 fusion.56
  46.0 23.0 %all_to_all.16 = f32[32,1,512]{2,1,0:T(1,128)S(1)} all-to-all(f32[32,1,512]{2,1,0:T(1,128)S(1)} %broadcast_in_dim.72), channel_id=1, replica_groups=mesh['curve'=32,'tm'=8] {'curve'}, dimensions={0} | all-to-all | bytes 131072 | tf_op jit(solution)/shard_map/all_to_all | solution.py:34
  69.0 0.1 reduce_sum.37
  69.1 0.0 copy-done
  69.1 0.5 fusion.37
  69.6 14.3 %all_to_all.17 = f32[8,256,64]{1,2,0:T(8,128)S(1)} all-to-all(f32[8,256,64]{1,2,0:T(8,128)S(1)} %broadcast_in_dim.73), channel_id=1, replica_groups=mesh['curve'=32,'tm'=8] {'tm'}, dimensions={0} | all-to-all | bytes 1048576 | tf_op jit(solution)/shard_map/all_to_all | solution.py:34
  84.0 0.0 copy-start.1
  84.0 0.7 convolution_multiply_fusion
  84.7 0.7 reshape.102
  85.5 5.6 %all-to-all-start.2 = ((f32[32,512,2]{1,2,0:T(2,128)}), f32[32,512,2]{1,2,0:T(2,128)S(1)}, u32[]{:S(2)}, u32[]{:S(2)}) async-start(f32[32,512,2]{1,2,0:T(2,128)} %bitcast.3), calls=%async_computation.2 | async-start | bytes 262144 | tf_op jit(solution)/shard_map/all_to_all | solution.py:48
  91.1 1.0 copy.26
  92.1 9.6 %all-to-all-done.2 = f32[32,512,2]{1,2,0:T(2,128)S(1)} async-done(((f32[32,512,2]{1,2,0:T(2,128)}), f32[32,512,2]{1,2,0:T(2,128)S(1)}, u32[]{:S(2)}, u32[]{:S(2)}) %all-to-all-start.2) | async-done | bytes 131104 | tf_op jit(solution)/shard_map/all_to_all | solution.py:48
  101.6 0.1 reduce_sum.39
  101.7 0.0 copy-done.3
  101.7 0.6 add.248
  102.3 0.0 copy-done.1
  (20 shorter events, 0.3 us)
Async XLA Ops:
  0.6 68.4 %copy-start = (f32[512,64]{0,1:T(8,128)S(1)}, f32[512,64]{0,1:T(8,128)}, u32[]{:S(2)}) copy-start(f32[512,64]{0,1:T(8,128)} %param.6) | copy-start | bytes 393220
  20.2 23.7 %copy-start.2 = (f32[256]{0:T(256)S(1)}, f32[256]{0:T(256)}, u32[]{:S(2)}) copy-start(f32[256]{0:T(256)} %param.5) | copy-start | bytes 3076
  31.7 7.5 %collective-permute-start.1 = (f32[256,3]{0,1:T(4,128)S(1)}, f32[256,3]{0,1:T(4,128)S(1)}, u32[]{:S(2)}, u32[]{:S(2)}) collective-permute-start(f32[256,3]{0,1:T(4,128)S(1)} %slice.196), channel_id=1, source_target_pairs={{0,1},{1,2},{2,3},{3,4},{4,5},{5,6},{6,7},{8,9},{9,10},{10,11},{11... | collective-permute-start | bytes 9224 | tf_op jit(solution)/shard_map/ppermute | solution.py:16
  35.7 4.9 %collective-permute-start = (f32[256,8]{0,1:T(8,128)S(1)}, f32[256,8]{0,1:T(8,128)S(1)}, u32[]{:S(2)}, u32[]{:S(2)}) collective-permute-start(f32[256,8]{0,1:T(8,128)S(1)} %slice.194), channel_id=1, source_target_pairs={{0,1},{1,2},{2,3},{3,4},{4,5},{5,6},{6,7},{8,9},{9,10},{10,11},{11... | collective-permute-start | bytes 24584 | tf_op jit(solution)/shard_map/ppermute | solution.py:24
  39.3 4.4 %collective-permute-start.2 = (f32[256,8]{0,1:T(8,128)S(1)}, f32[256,8]{0,1:T(8,128)S(1)}, u32[]{:S(2)}, u32[]{:S(2)}) collective-permute-start(f32[256,8]{0,1:T(8,128)S(1)} %fusion.41), channel_id=1, source_target_pairs={{1,0},{2,1},{3,2},{4,3},{5,4},{6,5},{7,6},{9,8},{10,9},{11,10},{12... | collective-permute-start | bytes 24584 | tf_op jit(solution)/shard_map/ppermute | solution.py:27
  44.7 57.0 %copy-start.3 = (f32[512,2]{0,1:T(2,128)S(1)}, f32[512,2]{0,1:T(2,128)}, u32[]{:S(2)}) copy-start(f32[512,2]{0,1:T(2,128)} %param.7) | copy-start | bytes 12292
  84.0 18.3 %copy-start.1 = (f32[256,64]{0,1:T(8,128)}, f32[256,64]{0,1:T(8,128)S(1)}, u32[]{:S(2)}) copy-start(f32[256,64]{0,1:T(8,128)S(1)} %reduce_sum.38) | copy-start | bytes 196612
  85.5 16.2 %all-to-all-start.2 = ((f32[32,512,2]{1,2,0:T(2,128)}), f32[32,512,2]{1,2,0:T(2,128)S(1)}, u32[]{:S(2)}, u32[]{:S(2)}) async-start(f32[32,512,2]{1,2,0:T(2,128)} %bitcast.3), calls=%async_computation.2 | async-start | bytes 262144 | tf_op jit(solution)/shard_map/all_to_all | solution.py:48
where the time goes:
time: 103 us; the launch traced here: 102 us
  blocking collectives  37.3 us (36%)
  local copies, waits for them, and re-layouts  21.8 us (21%)
  starting transfers between devices  13.9 us (13%)
  waiting for transfers between devices  12.7 us (12%)
  other arithmetic  8.06 us (8%)
  matrix products  7.67 us (7%)
    all_to_all x2, blocking collectives, sent_to_all(): return lax.all_to_all(copies, axis, split_axis=0, concat_axis=0, tiled=True)  37.3 us
    reshape x1, local copies, waits for them, and re-layouts, body(): blocks = samples.reshape(row_count, basis_width, SPB)  10.5 us
    unnamed x10, local copies, waits for them, and re-layouts  10.1 us
    all_to_all x1, waiting for transfers between devices, sent_and_summed(): lax.all_to_all(pieces, axis, split_axis=0, concat_axis=0, tiled=True)  9.59 us
    dot_general x1, matrix products, body(): jnp.einsum('cgq,mq->mcg', blocks, weight_table(), precision=lax.Precision...  6.42 us
    all_to_all x1, starting transfers between devices, sent_and_summed(): lax.all_to_all(pieces, axis, split_axis=0, concat_axis=0, tiled=True)  5.59 us
    add x1, other arithmetic, body(): padded[0, :, 0:basis_width + 3] + padded[1, :, 1:basis_width + 4]  4.7 us
    ppermute x1, starting transfers between devices, passed_along(): return lax.ppermute(block, axis, route)  3.94 us
  transfers between devices with their start and end apart: 4, of which 2 were waited for; matrix products, arithmetic and copies ran while one was open for 1% of the time, Pallas kernels for 0%

commit v1 on v0

v1 whole, which is shorter than its diff:
```python
import functools

import jax
import jax.numpy as jnp
import numpy as np
from jax import lax
from jax.experimental import pallas as pl
from jax.experimental.pallas import tpu as pltpu
from jax.sharding import PartitionSpec as P

SPB = 16
ITERS = 4
MARGIN = 2 * ITERS
LANES = 128
CHUNK = 1024
SEGS = CHUNK // SPB
SLOT = 16
GROUPS = LANES // SLOT
MESH = pl.DeviceIdType.MESH
damping = 0.45
TABLE_SCALE = 1.0 / (6.0 * 32.0**3 * SPB)


def banded_table():
    odd = 2 * np.arange(SPB, dtype=np.int64) + 1
    pieces = np.stack(
        [
            odd**3,
            -3 * odd**3 + 96 * odd**2 + 3072 * odd + 32768,
            3 * odd**3 - 192 * odd**2 + 4 * 32768,
            (32 - odd) ** 3,
        ]
    )
    band = np.zeros((CHUNK, LANES), np.float64)
    for segment in range(SEGS):
        for m in range(4):
            band[segment * SPB : (segment + 1) * SPB, segment + 3 - m] = pieces[m]
    high = band.astype(jnp.bfloat16)
    low = (band - high.astype(np.float64)).astype(jnp.bfloat16)
    return np.concatenate([high, low], axis=1)


def roll(value, shift):
    return pltpu.roll(value, shift % LANES, 1)


def kernel(
    curves,
    blocks,
    x_hbm,
    s_ref,
    tt_ref,
    prev_ref,
    w_hbm,
    coef_ref,
    score_ref,
    sketch_ref,
    xbuf,
    wbuf,
    obuf,
    smooth,
    to_left,
    to_right,
    from_left,
    from_right,
    local,
    msend,
    mall,
    lsend,
    lparts,
    lfull,
    usend,
    uparts,
    spack,
    sparts,
    x_sem,
    w_sem,
    halo_send,
    halo_recv,
    m_send,
    m_recv,
    rs_send,
    rs_recv,
    ag_send,
    ag_recv,
    u_send,
    u_recv,
    f_send,
    f_recv,
):
    rows, width = coef_ref.shape
    tiles = width // LANES
    chunks = x_hbm.shape[1] // CHUNK
    group = rows // GROUPS
    rank = tt_ref.shape[0]
    share = rank // blocks
    owned = rank // curves * tiles
    cg, tb = lax.axis_index("curve"), lax.axis_index("tm")
    left, right = lax.rem(tb + blocks - 1, blocks), lax.rem(tb + 1, blocks)

    def fetch(c):
        return pltpu.make_async_copy(x_hbm.at[:, pl.ds(c * CHUNK, CHUNK)], xbuf.at[c], x_sem.at[c])

    table_copy = pltpu.make_async_copy(w_hbm, wbuf, w_sem)
    fetch(0).start()
    table_copy.start()
    fetch(chunks - 1).start()
    for c in range(1, chunks - 1):
        fetch(c).start()

    barrier = pltpu.get_barrier_semaphore()

    @pl.loop(1, blocks)
    def _(k):
        pl.semaphore_signal(
            barrier, inc=1, device_id={"tm": lax.rem(tb + k, blocks)}, device_id_type=MESH
        )

    @pl.loop(1, curves)
    def _(k):
        pl.semaphore_signal(
            barrier, inc=1, device_id={"curve": lax.rem(cg + k, curves)}, device_id_type=MESH
        )

    line = s_ref.shape[1]
    for i in range(rows // line):
        smooth[pl.ds(i * line, line), :] = jnp.transpose(
            jnp.broadcast_to(s_ref[i : i + 1, :], (LANES, line))
        )

    def project(c):
        fetch(c).wait()
        x = xbuf[c]
        high = x.astype(jnp.bfloat16)
        rest = x - high.astype(jnp.float32)
        middle = rest.astype(jnp.bfloat16)
        low = (rest - middle.astype(jnp.float32)).astype(jnp.bfloat16)
        w = wbuf[...]
        total = jnp.dot(high, w, preferred_element_type=jnp.float32)
        total += jnp.dot(middle, w, preferred_element_type=jnp.float32)
        total += jnp.dot(low, w, preferred_element_type=jnp.float32)
        obuf[c] = (total[:, :LANES] + total[:, LANES:]) * TABLE_SCALE

    lane = lax.broadcasted_iota(jnp.int32, (group, LANES), 1)
    table_copy.wait()
    project(0)
    project(chunks - 1)
    packed_left = jnp.zeros((group, LANES), jnp.float32)
    packed_right = jnp.zeros((group, LANES), jnp.float32)
    last = SEGS - MARGIN
    for g in range(GROUPS):
        here = (lane >= g * SLOT) & (lane < (g + 1) * SLOT)
        at = pl.ds(g * group, group)
        packed_left = jnp.where(here, roll(obuf[0, at, :], g * SLOT), packed_left)
        packed_right = jnp.where(here, roll(obuf[chunks - 1, at, :], g * SLOT - last), packed_right)
    to_left[...] = packed_left
    to_right[...] = packed_right

    pl.semaphore_wait(barrier, blocks + curves - 2)

    def halo(side, source, target, device):
        return pltpu.make_async_remote_copy(
            src_ref=source,
            dst_ref=target,
            send_sem=halo_send.at[side],
            recv_sem=halo_recv.at[side],
            device_id={"tm": device},
            device_id_type=MESH,
        )

    send_left = halo(0, to_left, from_right, left)
    send_right = halo(1, to_right, from_left, right)
    send_left.start()
    send_right.start()

    @pl.loop(1, chunks - 1)
    def _(c):
        project(c)

    send_left.wait()
    send_right.wait()

    zero = jnp.zeros((), jnp.float32)
    has_left = jnp.where(tb > 0, 1.0, zero)
    has_right = jnp.where(tb < blocks - 1, 1.0, zero)
    first, final = tb == 0, tb == blocks - 1
    upper = lane >= LANES // 2

    def relax(g, sums):
        at = pl.ds(pl.multiple_of(g * group, group), group)
        arrived_left = pltpu.roll(from_left[...], lax.rem(LANES - MARGIN + LANES - g * SLOT, LANES), 1)
        arrived_right = pltpu.roll(from_right[...], lax.rem(LANES - g * SLOT, LANES), 1)
        arrived_left = arrived_left * has_left
        arrived_right = arrived_right * has_right
        spill = jnp.where(lane < 3, arrived_left, 0.0)
        target = []
        for i in range(tiles):
            odd = roll(obuf[2 * i + 1, at, :], LANES // 2)
            target.append(obuf[2 * i, at, :] + jnp.where(upper, odd, spill))
            spill = jnp.where(upper, 0.0, odd)
        outside = jnp.where(lane < MARGIN, arrived_right + spill, 0.0)
        target.append(jnp.where(lane >= LANES - MARGIN, arrived_left, outside))
        s = smooth[at, :]
        inner = damping / (1.0 + 6.0 * s)
        near = damping / (1.0 + 5.0 * s)
        edge = damping / (1.0 + s)
        step = [inner] * (tiles + 1)
        low_step = jnp.where(first & (lane == 0), edge, jnp.where(first & (lane == 1), near, step[0]))
        step[0] = low_step
        top = LANES - 1
        step[tiles - 1] = jnp.where(
            final & (lane == top), edge, jnp.where(final & (lane == top - 1), near, step[tiles - 1])
        )
        pull = [a * p for a, p in zip(step, target)]
        keep = [1.0 - a for a in step]
        bend = [a * s for a in step]
        count = tiles + 1

        def spread(values):
            up = [roll(v, -1) for v in values]
            down = [roll(v, 1) for v in values]
            out = []
            for i in range(count):
                nxt = jnp.where(lane == LANES - 1, up[(i + 1) % count], up[i])
                prv = jnp.where(lane == 0, down[(i - 1) % count], down[i])
                out.append(nxt + prv - 2.0 * values[i])
            return out

        c = target
        for _ in range(ITERS):
            second = spread(c)
            second[0] = jnp.where(first & (lane == 0), 0.0, second[0])
            second[tiles - 1] = jnp.where(final & (lane == LANES - 1), 0.0, second[tiles - 1])
            second[tiles] = jnp.where(
                (first & (lane == LANES - 1)) | (final & (lane == 0)), 0.0, second[tiles]
            )
            fourth = spread(second)
            c = [keep[i] * c[i] + pull[i] - bend[i] * fourth[i] for i in range(count)]
        out = []
        for i in range(tiles):
            coef_ref[at, pl.ds(i * LANES, LANES)] = c[i]
            out.append(sums[i] + c[i])
        return tuple(out)

    start = tuple(jnp.zeros((group, LANES), jnp.float32) for _ in range(tiles))
    sums = lax.fori_loop(0, GROUPS, relax, start)
    own_mean = [jnp.sum(v, axis=0, keepdims=True) / rows for v in sums]

    msend[...] = jnp.zeros_like(msend)
    for i in range(tiles):
        msend[i : i + 1, :] = own_mean[i]

    def mean_copy(k):
        return pltpu.make_async_remote_copy(
            src_ref=msend,
            dst_ref=mall.at[cg],
            send_sem=m_send.at[k],
            recv_sem=m_recv.at[k],
            device_id={"curve": lax.rem(cg + k, curves)},
            device_id_type=MESH,
        )

    @pl.loop(1, curves)
    def _(k):
        mean_copy(k).start()

    mall[cg] = msend[...]

    mean_row = jnp.concatenate(own_mean, axis=1)
    centred = coef_ref[...] - mean_row
    local[...] = centred
    stacked = jnp.concatenate([centred, jnp.broadcast_to(mean_row, (LANES, width))], axis=0)
    contract_last = (((1,), (1,)), ((), ()))
    partial = lax.dot_general(
        tt_ref[...],
        stacked,
        contract_last,
        precision=lax.Precision.HIGHEST,
        preferred_element_type=jnp.float32,
    )
    lsend[...] = partial.reshape(blocks, share, rows + LANES)

    def scatter_copy(k):
        to = lax.rem(tb + k, blocks)
        return pltpu.make_async_remote_copy(
            src_ref=lsend.at[to],
            dst_ref=lparts.at[tb],
            send_sem=rs_send.at[k],
            recv_sem=rs_recv.at[k],
            device_id={"tm": to},
            device_id_type=MESH,
        )

    def gather_copy(k):
        return pltpu.make_async_remote_copy(
            src_ref=lfull.at[tb],
            dst_ref=lfull.at[tb],
            send_sem=ag_send.at[k],
            recv_sem=ag_recv.at[k],
            device_id={"tm": lax.rem(tb + k, blocks)},
            device_id_type=MESH,
        )

    def shift_copy(k):
        return pltpu.make_async_remote_copy(
            src_ref=usend,
            dst_ref=uparts.at[tb],
            send_sem=u_send.at[k],
            recv_sem=u_recv.at[k],
            device_id={"tm": lax.rem(tb + k, blocks)},
            device_id_type=MESH,
        )

    def sketch_copy(k):
        to = lax.rem(cg + k, curves)
        return pltpu.make_async_remote_copy(
            src_ref=spack.at[pl.ds(pl.multiple_of(to * owned, owned), owned), :],
            dst_ref=sparts.at[cg],
            send_sem=f_send.at[k],
            recv_sem=f_recv.at[k],
            device_id={"curve": to},
            device_id_type=MESH,
        )

    @pl.loop(1, blocks)
    def _(k):
        scatter_copy(k).start()

    lparts[tb] = lsend[tb]

    @pl.loop(1, blocks)
    def _(k):
        scatter_copy(k).wait()

    lfull[tb] = jnp.sum(lparts[...], axis=0)

    @pl.loop(1, blocks)
    def _(k):
        gather_copy(k).start()

    @pl.loop(1, curves)
    def _(k):
        mean_copy(k).wait()

    means = mall[...]
    rough = jnp.sum(means, axis=0) / curves
    slip = jnp.sum(means - rough[None], axis=0) / curves
    apart = (msend[...] - rough) - slip
    apart_row = jnp.concatenate(
        [jnp.broadcast_to(apart[i : i + 1, :], (8, LANES)) for i in range(tiles)], axis=1
    )
    shift_part = lax.dot_general(
        apart_row,
        tt_ref[...],
        contract_last,
        precision=lax.Precision.HIGHEST,
        preferred_element_type=jnp.float32,
    )
    usend[...] = jnp.zeros_like(usend)
    usend[:, pl.ds(0, rank)] = shift_part

    @pl.loop(1, blocks)
    def _(k):
        shift_copy(k).start()

    uparts[tb] = usend[...]

    @pl.loop(1, blocks)
    def _(k):
        gather_copy(k).wait()

    full = lfull[...].reshape(rank, rows + LANES)
    inner_scores = full[:, :rows]
    group_scores = full[:, rows:]
    part = jnp.dot(
        inner_scores,
        local[...],
        precision=lax.Precision.HIGHEST,
        preferred_element_type=jnp.float32,
    )
    for i in range(tiles):
        between = group_scores * (float(rows) * apart[i : i + 1, :])
        spack[pl.ds(i, rank, stride=tiles), :] = part[:, i * LANES : (i + 1) * LANES] + between

    @pl.loop(1, curves)
    def _(k):
        sketch_copy(k).start()

    sparts[cg] = spack[pl.ds(pl.multiple_of(cg * owned, owned), owned), :]

    @pl.loop(1, blocks)
    def _(k):
        shift_copy(k).wait()

    shift = jnp.sum(uparts[...], axis=0)
    shift_col = jnp.transpose(jnp.broadcast_to(shift[0:1, :], (LANES, LANES)))[:rank, :1]
    score_ref[...] = inner_scores + shift_col

    @pl.loop(1, curves)
    def _(k):
        sketch_copy(k).wait()

    total = jnp.sum(sparts[...], axis=0) / (rows * curves)
    for p in range(rank // curves):
        for i in range(tiles):
            at = pl.ds(i * LANES, LANES)
            row = p * tiles + i
            sketch_ref[p : p + 1, at] = prev_ref[p : p + 1, at] + total[row : row + 1, :]


def body(curves, blocks, samples, smoothing, test_matrix, sketch_prev):
    rows, taken = samples.shape
    width = taken // SPB
    rank = test_matrix.shape[1]
    tiles = width // LANES
    chunks = taken // CHUNK
    group = rows // GROUPS
    share = rank // blocks
    owned = rank // curves * tiles
    line = min(rows, LANES)
    f32 = jnp.float32
    vmem = pl.BlockSpec(memory_space=pltpu.VMEM)
    anywhere = pl.BlockSpec(memory_space=pl.ANY)
    dma = pltpu.SemaphoreType.DMA
    coef, score_t, sketch_t = pl.pallas_call(
        functools.partial(kernel, curves, blocks),
        out_shape=(
            jax.ShapeDtypeStruct((rows, width), f32),
            jax.ShapeDtypeStruct((rank, rows), f32),
            jax.ShapeDtypeStruct((rank // curves, width), f32),
        ),
        in_specs=[anywhere, vmem, vmem, vmem, anywhere],
        out_specs=(vmem, vmem, vmem),
        scratch_shapes=[
            pltpu.VMEM((chunks, rows, CHUNK), f32),
            pltpu.VMEM((CHUNK, 2 * LANES), jnp.bfloat16),
            pltpu.VMEM((chunks, rows, LANES), f32),
            pltpu.VMEM((rows, LANES), f32),
            pltpu.VMEM((group, LANES), f32),
            pltpu.VMEM((group, LANES), f32),
            pltpu.VMEM((group, LANES), f32),
            pltpu.VMEM((group, LANES), f32),
            pltpu.VMEM((rows, width), f32),
            pltpu.VMEM((8, LANES), f32),
            pltpu.VMEM((curves, 8, LANES), f32),
            pltpu.VMEM((blocks, share, rows + LANES), f32),
            pltpu.VMEM((blocks, share, rows + LANES), f32),
            pltpu.VMEM((blocks, share, rows + LANES), f32),
            pltpu.VMEM((8, LANES), f32),
            pltpu.VMEM((blocks, 8, LANES), f32),
            pltpu.VMEM((rank * tiles, LANES), f32),
            pltpu.VMEM((curves, owned, LANES), f32),
            dma((chunks,)),
            dma,
            dma((2,)),
            dma((2,)),
            dma((curves,)),
            dma((curves,)),
            dma((blocks,)),
            dma((blocks,)),
            dma((blocks,)),
            dma((blocks,)),
            dma((blocks,)),
            dma((blocks,)),
            dma((curves,)),
            dma((curves,)),
        ],
        compiler_params=pltpu.CompilerParams(
            collective_id=0, has_side_effects=True, vmem_limit_bytes=48 * 1024 * 1024
        ),
    )(
        samples,
        smoothing.reshape(rows // line, line),
        test_matrix.T,
        sketch_prev.T,
        jnp.asarray(banded_table()),
    )
    return coef, score_t.T, sketch_t.T


def solution(mesh):
    placed = (P("curve", "tm"), P("curve"), P("tm", None), P("tm", "curve"))
    return jax.shard_map(
        functools.partial(body, mesh.shape["curve"], mesh.shape["tm"]),
        mesh=mesh,
        in_specs=placed,
        out_specs=(P("curve", "tm"), P("curve", None), P("tm", "curve")),
        check_vma=False,
    )
```

time: 103 us -> 47.2 us (0.46)
  Pallas kernels: 0 us -> 41.1 us
  blocking collectives: 37.3 us -> 0 us
  local copies, waits for them, and re-layouts: 21.8 us -> 5.32 us
  starting transfers between devices: 13.9 us -> 0 us
  waiting for transfers between devices: 12.7 us -> 0 us
  other arithmetic: 8.06 us -> 0 us
  matrix products: 7.67 us -> 0 us
    pallas_call x0 -> x1, Pallas kernels: none -> 41.1 us  [body(): pl.pallas_call(functools.partial(kernel, curves, blocks), out_shape=(jax....]
    all_to_all x2 -> x0, blocking collectives: 37.3 us -> none  [sent_to_all(): return lax.all_to_all(copies, axis, split_axis=0, concat_axis=0, tiled=True)]
    reshape x2 -> x0, local copies, waits for them, and re-layouts: 11.2 us -> none  [the longest x1 10.5 us: body(): blocks = samples.reshape(row_count, basis_width, SPB)]
    all_to_all x1 -> x0, waiting for transfers between devices: 9.59 us -> none  [sent_and_summed(): lax.all_to_all(pieces, axis, split_axis=0, concat_axis=0, tiled=True)]
    ppermute x3 -> x0, starting transfers between devices: 8.34 us -> none  [the longest x1 3.94 us: passed_along(): return lax.ppermute(block, axis, route)]
    dot_general x3 -> x0, matrix products: 7.67 us -> none  [the longest x1 6.42 us: body(): jnp.einsum('cgq,mq->mcg', blocks, weight_table(), precision=lax.Precision...]
    add x14 -> x0, other arithmetic: 6.67 us -> none  [the longest x1 4.7 us: body(): padded[0, :, 0:basis_width + 3] + padded[1, :, 1:basis_width + 4]]
    all_to_all x1 -> x0, starting transfers between devices: 5.59 us -> none  [sent_and_summed(): lax.all_to_all(pieces, axis, split_axis=0, concat_axis=0, tiled=True)]
  transfers between devices with their start and end apart: 4 -> 0, of which waited for: 2 -> 0; matrix products, arithmetic and copies ran while one was open for 1% -> 0% of each run, Pallas kernels for 0% -> 0%
where the time goes in v1:
time: 47.2 us; the launch traced here: 47 us
  Pallas kernels  41.1 us (87%)
  local copies, waits for them, and re-layouts  5.32 us (11%)
  between operations  0.65 us (1%)
    pallas_call x1, Pallas kernels, body(): pl.pallas_call(functools.partial(kernel, curves, blocks), out_shape=(jax....  41.1 us
    unnamed x11, local copies, waits for them, and re-layouts  5.32 us

profile of v1, /device:TPU:1, one launch (start us, length us, event | category | flops | bytes accessed | tf_op | source)
XLA Modules:
  0.0 47.0 jit_solution(13805998687339261335)
XLA Ops:
  0.6 0.0 copy-start
  0.6 1.0 %copy-done = bf16[1024,256]{1,0:T(8,128)(2,1)S(1)} copy-done((bf16[1024,256]{1,0:T(8,128)(2,1)S(1)}, bf16[1024,256]{1,0:T(8,128)(2,1)}, u32[]{:S(2)}) %copy-start) | copy-done | bytes 524312
  1.7 0.0 copy-start.1
  1.7 0.9 %copy-done.1 = f32[512,64]{0,1:T(8,128)S(1)} copy-done((f32[512,64]{0,1:T(8,128)S(1)}, f32[512,64]{0,1:T(8,128)}, u32[]{:S(2)}) %copy-start.1) | copy-done | bytes 131096
  2.6 0.0 copy-start.2
  2.6 0.7 %copy-done.2 = f32[512,2]{0,1:T(2,128)S(1)} copy-done((f32[512,2]{0,1:T(2,128)S(1)}, f32[512,2]{0,1:T(2,128)}, u32[]{:S(2)}) %copy-start.2) | copy-done | bytes 4120
  3.3 0.0 copy-start.3
  3.3 0.7 %copy-done.3 = f32[256]{0:T(256)S(1)} copy-done((f32[256]{0:T(256)S(1)}, f32[256]{0:T(256)}, u32[]{:S(2)}) %copy-start.3) | copy-done | bytes 1048
  3.9 41.1 %shard_map.76 = (f32[256,512]{1,0:T(8,128)S(1)}, f32[64,256]{1,0:T(8,128)S(1)}, f32[2,512]{1,0:T(2,128)S(1)}) custom-call(f32[256,8192]{1,0:T(8,128)} %x_hbm.1, f32[2,128]{1,0:T(2,128)S(1)} %bitcast.9, f32[64,512]{1,0:T(8,128)S(1)} %bitcast.5, f32[2,512]{1,0:T(2,128)S(1)} %bitcast.7, bf16[1024,256]{1,0:T(8,128)(2,1)S(1)} %copy-done), custom_call_target="tpu_custom_call" | custom-call | tf_op jit(solution)/shard_map/pallas_call | solution.py:425
  45.0 0.8 %copy.11 = f32[256,512]{1,0:T(8,128)} copy(f32[256,512]{1,0:T(8,128)S(1)} %get-tuple-element.12) | data formatting | bytes 1048576
  45.8 0.6 %copy.12 = f32[256,64]{0,1:T(8,128)} copy(f32[256,64]{0,1:T(8,128)S(1)} %bitcast.6) | data formatting | bytes 131072
  46.5 0.6 %copy.13 = f32[512,2]{0,1:T(2,128)} copy(f32[512,2]{0,1:T(2,128)S(1)} %bitcast.8) | data formatting | bytes 8192
Async XLA Ops:
  0.6 1.0 %copy-start = (bf16[1024,256]{1,0:T(8,128)(2,1)S(1)}, bf16[1024,256]{1,0:T(8,128)(2,1)}, u32[]{:S(2)}) copy-start(bf16[1024,256]{1,0:T(8,128)(2,1)} %constant.2.clone.w_hbm) | copy-start | bytes 1572868
  1.7 0.9 %copy-start.1 = (f32[512,64]{0,1:T(8,128)S(1)}, f32[512,64]{0,1:T(8,128)}, u32[]{:S(2)}) copy-start(f32[512,64]{0,1:T(8,128)} %param.7) | copy-start | bytes 393220
  2.6 0.7 %copy-start.2 = (f32[512,2]{0,1:T(2,128)S(1)}, f32[512,2]{0,1:T(2,128)}, u32[]{:S(2)}) copy-start(f32[512,2]{0,1:T(2,128)} %param.8) | copy-start | bytes 12292
  3.3 0.7 %copy-start.3 = (f32[256]{0:T(256)S(1)}, f32[256]{0:T(256)}, u32[]{:S(2)}) copy-start(f32[256]{0:T(256)} %param.6) | copy-start | bytes 3076

commit v2 on v1

v2 whole, which is shorter than its diff:
```python
import functools

import jax
import jax.numpy as jnp
import numpy as np
from jax import lax
from jax.experimental import pallas as pl
from jax.experimental.pallas import tpu as pltpu
from jax.sharding import PartitionSpec as P

SPB = 16
ITERS = 4
MARGIN = 2 * ITERS
LANES = 128
TILE = 8
CHUNK = 1024
SEGS = CHUNK // SPB
SPAN = SEGS + TILE
MESH = pl.DeviceIdType.MESH
CONTRACT_LAST = (((1,), (1,)), ((), ()))
damping = 0.45
TABLE_SCALE = 1.0 / (6.0 * 32.0**3 * SPB)


def banded_table():
    odd = 2 * np.arange(SPB, dtype=np.int64) + 1
    pieces = np.stack(
        [
            odd**3,
            -3 * odd**3 + 96 * odd**2 + 3072 * odd + 32768,
            3 * odd**3 - 192 * odd**2 + 4 * 32768,
            (32 - odd) ** 3,
        ]
    )
    band = np.zeros((SPAN, CHUNK), np.float64)
    for segment in range(SEGS):
        for m in range(4):
            band[segment + 3 - m, segment * SPB : (segment + 1) * SPB] = pieces[m]
    high = band.astype(jnp.bfloat16)
    low = (band - high.astype(np.float64)).astype(jnp.bfloat16)
    return np.concatenate([high, low], axis=0)


def split(value):
    high = value.astype(jnp.bfloat16)
    rest = value - high.astype(jnp.float32)
    middle = rest.astype(jnp.bfloat16)
    low = (rest - middle.astype(jnp.float32)).astype(jnp.bfloat16)
    return high, middle, low


def stacked_dot(parts, count, other, transposed):
    total = None
    for used, right in zip((3, 2, 1), other):
        left = parts[: used * count]
        if transposed:
            out = lax.dot_general(left, right, CONTRACT_LAST, preferred_element_type=jnp.float32)
        else:
            out = jnp.dot(left, right, preferred_element_type=jnp.float32)
        for i in range(used):
            piece = out[i * count : (i + 1) * count]
            total = piece if total is None else total + piece
    return total


def kernel(
    curves,
    blocks,
    x_hbm,
    s_hbm,
    tt_hbm,
    prev_hbm,
    w_hbm,
    coef_ref,
    score_ref,
    sketch_ref,
    xbuf,
    wbuf,
    sbuf,
    ttbuf,
    prevbuf,
    obuf,
    from_left,
    from_right,
    target,
    even,
    uneven,
    parts,
    msend,
    mall,
    lsend,
    lparts,
    lfull,
    usend,
    uparts,
    spack,
    sparts,
    x_sem,
    in_sem,
    halo_send,
    halo_recv,
    m_send,
    m_recv,
    rs_send,
    rs_recv,
    ag_send,
    ag_recv,
    u_send,
    u_recv,
    f_send,
    f_recv,
):
    rows, width = coef_ref.shape
    halves = rows // LANES
    tiles = width // LANES
    chunks = x_hbm.shape[1] // CHUNK
    rank = tt_hbm.shape[0]
    share = rank // blocks
    owned = rank // curves * tiles
    cg, tb = lax.axis_index("curve"), lax.axis_index("tm")
    left, right = lax.rem(tb + blocks - 1, blocks), lax.rem(tb + 1, blocks)

    def fetch(c):
        return pltpu.make_async_copy(x_hbm.at[:, pl.ds(c * CHUNK, CHUNK)], xbuf.at[c], x_sem.at[c])

    table_copy = pltpu.make_async_copy(w_hbm, wbuf, in_sem.at[0])
    small = [
        pltpu.make_async_copy(s_hbm, sbuf, in_sem.at[1]),
        pltpu.make_async_copy(tt_hbm, ttbuf, in_sem.at[2]),
        pltpu.make_async_copy(prev_hbm, prevbuf, in_sem.at[3]),
    ]
    table_copy.start()
    fetch(0).start()
    fetch(chunks - 1).start()
    for c in range(1, chunks - 1):
        fetch(c).start()
    for copy in small:
        copy.start()

    barrier = pltpu.get_barrier_semaphore()

    @pl.loop(1, blocks)
    def _(k):
        pl.semaphore_signal(
            barrier, inc=1, device_id={"tm": lax.rem(tb + k, blocks)}, device_id_type=MESH
        )

    @pl.loop(1, curves)
    def _(k):
        pl.semaphore_signal(
            barrier, inc=1, device_id={"curve": lax.rem(cg + k, curves)}, device_id_type=MESH
        )

    def project(c):
        fetch(c).wait()
        w = wbuf[...]
        total = None
        for part in split(xbuf[c]):
            out = lax.dot_general(w, part, CONTRACT_LAST, preferred_element_type=jnp.float32)
            total = out if total is None else total + out
        total = (total[:SPAN] + total[SPAN:]) * TABLE_SCALE
        for h in range(halves):
            obuf[c, h] = total[:, h * LANES : (h + 1) * LANES]

    table_copy.wait()
    project(0)
    project(chunks - 1)

    pl.semaphore_wait(barrier, blocks + curves - 2)

    def halo(side, source, to, device):
        return pltpu.make_async_remote_copy(
            src_ref=source,
            dst_ref=to,
            send_sem=halo_send.at[side],
            recv_sem=halo_recv.at[side],
            device_id={"tm": device},
            device_id_type=MESH,
        )

    edge_low = obuf.at[0, :, pl.ds(0, MARGIN), :]
    edge_high = obuf.at[chunks - 1, :, pl.ds(SEGS - MARGIN, 2 * MARGIN), :]
    send_left = halo(0, edge_low, from_right, left)
    send_right = halo(1, edge_high, from_left, right)
    send_left.start()
    send_right.start()

    @pl.loop(1, chunks - 1)
    def _(c):
        project(c)

    for copy in small:
        copy.wait()
    first, final = tb == 0, tb == blocks - 1
    row = lax.broadcasted_iota(jnp.int32, (TILE, LANES), 0)
    own = 2 * TILE
    size = width + 4 * TILE
    blank = jnp.zeros((TILE, LANES), jnp.float32)

    for buffer in (target, even, uneven):
        for h in range(halves):
            buffer[h, pl.ds(0, TILE), :] = blank
            buffer[h, pl.ds(size - TILE, TILE), :] = blank

    def put(h, at, value):
        target[h, at, :] = value
        even[h, at, :] = value

    for h in range(halves):
        for c in range(1, chunks):
            start = own + c * SEGS
            put(h, pl.ds(start, TILE), obuf[c, h, 0:TILE, :] + obuf[c - 1, h, SEGS:SPAN, :])
            put(h, pl.ds(start + TILE, SEGS - TILE), obuf[c, h, TILE:SEGS, :])
        put(h, pl.ds(own + TILE, SEGS - TILE), obuf[0, h, TILE:SEGS, :])

    send_left.wait()
    send_right.wait()
    for h in range(halves):
        halo_low = jnp.where(first, 0.0, from_left[h, 0:MARGIN, :])
        spilled = jnp.where(first, 0.0, from_left[h, MARGIN : 2 * MARGIN, :])
        halo_high = jnp.where(final, 0.0, from_right[h])
        put(h, pl.ds(own - TILE, TILE), halo_low)
        put(h, pl.ds(own, TILE), obuf[0, h, 0:TILE, :] + spilled)
        put(h, pl.ds(own + width, TILE), halo_high + obuf[chunks - 1, h, SEGS:SPAN, :])

    low_0, low_1 = first & (row == 0), first & (row == 1)
    top_0, top_1 = final & (row == TILE - 1), final & (row == TILE - 2)

    def sweep(source, result):
        for h in range(halves):
            s = jnp.broadcast_to(sbuf[h : h + 1, :], (TILE, LANES))
            inner = damping / (1.0 + 6.0 * s)
            near = damping / (1.0 + 5.0 * s)
            edge = damping / (1.0 + s)

            def moved(start, count, by):
                return source[h, pl.ds(start + by, count), :]

            def outer(start, count, off, rate, weight):
                pull = target[h, pl.ds(start, count), :] - weight * off
                value = (1.0 - damping) * moved(start, count, 0) + rate * pull
                result[h, pl.ds(start, count), :] = value

            def plain(start, count):
                far = moved(start, count, -2) + moved(start, count, 2)
                near_by = moved(start, count, -1) + moved(start, count, 1)
                grow = count // TILE
                rate = jnp.concatenate([inner] * grow, axis=0) if grow > 1 else inner
                weight = jnp.concatenate([s] * grow, axis=0) if grow > 1 else s
                outer(start, count, far - 4.0 * near_by, rate, weight)

            start = own
            below_2 = jnp.where(low_0 | low_1, 0.0, moved(start, TILE, -2))
            below_1 = jnp.where(low_0, 0.0, jnp.where(low_1, 2.0, 4.0) * moved(start, TILE, -1))
            above_1 = jnp.where(low_0, 2.0, 4.0) * moved(start, TILE, 1)
            off = below_2 + moved(start, TILE, 2) - (below_1 + above_1)
            outer(start, TILE, off, jnp.where(low_0, edge, jnp.where(low_1, near, inner)), s)
            start = own + width - TILE
            above_2 = jnp.where(top_0 | top_1, 0.0, moved(start, TILE, 2))
            above_1 = jnp.where(top_0, 0.0, jnp.where(top_1, 2.0, 4.0) * moved(start, TILE, 1))
            below_1 = jnp.where(top_0, 2.0, 4.0) * moved(start, TILE, -1)
            off = above_2 + moved(start, TILE, -2) - (below_1 + above_1)
            outer(start, TILE, off, jnp.where(top_0, edge, jnp.where(top_1, near, inner)), s)

            plain(own - TILE, TILE)
            plain(own + width, TILE)
            for start in range(own + TILE, own + width - TILE, TILE):
                plain(start, TILE)

    sweep(even, uneven)
    sweep(uneven, even)
    sweep(even, uneven)
    sweep(uneven, even)

    for h in range(halves):
        at = pl.ds(h * LANES, LANES)
        for i, part in enumerate(split(even[h, pl.ds(own, width), :])):
            parts[i, :, at] = part
    tt = ttbuf[...]
    tt_parts = jnp.concatenate(split(tt), axis=0)
    partial = stacked_dot(tt_parts, rank, [parts[i] for i in range(3)], False)
    lsend[...] = partial.reshape(blocks, share, rows)

    def scatter_copy(k):
        to = lax.rem(tb + k, blocks)
        return pltpu.make_async_remote_copy(
            src_ref=lsend.at[to],
            dst_ref=lparts.at[tb],
            send_sem=rs_send.at[k],
            recv_sem=rs_recv.at[k],
            device_id={"tm": to},
            device_id_type=MESH,
        )

    def gather_copy(k):
        return pltpu.make_async_remote_copy(
            src_ref=lfull.at[tb],
            dst_ref=lfull.at[tb],
            send_sem=ag_send.at[k],
            recv_sem=ag_recv.at[k],
            device_id={"tm": lax.rem(tb + k, blocks)},
            device_id_type=MESH,
        )

    def shift_copy(k):
        return pltpu.make_async_remote_copy(
            src_ref=usend,
            dst_ref=uparts.at[tb],
            send_sem=u_send.at[k],
            recv_sem=u_recv.at[k],
            device_id={"tm": lax.rem(tb + k, blocks)},
            device_id_type=MESH,
        )

    def mean_copy(k):
        return pltpu.make_async_remote_copy(
            src_ref=msend,
            dst_ref=mall.at[cg],
            send_sem=m_send.at[k],
            recv_sem=m_recv.at[k],
            device_id={"curve": lax.rem(cg + k, curves)},
            device_id_type=MESH,
        )

    def sketch_copy(k):
        to = lax.rem(cg + k, curves)
        return pltpu.make_async_remote_copy(
            src_ref=spack.at[pl.ds(pl.multiple_of(to * owned, owned), owned), :],
            dst_ref=sparts.at[cg],
            send_sem=f_send.at[k],
            recv_sem=f_recv.at[k],
            device_id={"curve": to},
            device_id_type=MESH,
        )

    @pl.loop(1, blocks)
    def _(k):
        scatter_copy(k).start()

    lparts[tb] = lsend[tb]

    lane = lax.broadcasted_iota(jnp.int32, (LANES, LANES), 1)
    line = lax.broadcasted_iota(jnp.int32, (LANES, LANES), 0)
    msend[...] = jnp.zeros_like(msend)
    for i in range(tiles):
        at = pl.ds(own + i * LANES, LANES)
        block = even[0, at, :]
        for h in range(1, halves):
            block += even[h, at, :]
        mean = jnp.sum(block, axis=1, keepdims=True) / rows
        msend[i : i + 1, :] = jnp.sum(jnp.where(lane == line, mean, 0.0), axis=0, keepdims=True)

    @pl.loop(1, curves)
    def _(k):
        mean_copy(k).start()

    mall[cg] = msend[...]

    for h in range(halves):
        for i in range(tiles):
            block = even[h, pl.ds(own + i * LANES, LANES), :]
            coef_ref[pl.ds(h * LANES, LANES), pl.ds(i * LANES, LANES)] = jnp.transpose(block)

    @pl.loop(1, blocks)
    def _(k):
        scatter_copy(k).wait()

    mine = jnp.sum(lparts[...], axis=0)
    group_score = jnp.sum(mine, axis=1, keepdims=True) / rows
    mine = mine - group_score
    slip = jnp.sum(mine, axis=1, keepdims=True) / rows
    lfull[tb] = jnp.concatenate(
        [mine - slip, jnp.broadcast_to(group_score + slip, (share, LANES))], axis=1
    )

    @pl.loop(1, blocks)
    def _(k):
        gather_copy(k).start()

    @pl.loop(1, curves)
    def _(k):
        mean_copy(k).wait()

    means = mall[...]
    rough = jnp.sum(means, axis=0) / curves
    slip = jnp.sum(means - rough[None], axis=0) / curves
    apart = (msend[...] - rough) - slip
    apart_row = jnp.concatenate(
        [jnp.broadcast_to(apart[i : i + 1, :], (TILE, LANES)) for i in range(tiles)], axis=1
    )
    shift_part = lax.dot_general(
        apart_row,
        tt,
        CONTRACT_LAST,
        precision=lax.Precision.HIGHEST,
        preferred_element_type=jnp.float32,
    )
    usend[...] = jnp.zeros_like(usend)
    usend[:, pl.ds(0, rank)] = shift_part

    @pl.loop(1, blocks)
    def _(k):
        shift_copy(k).start()

    uparts[tb] = usend[...]

    @pl.loop(1, blocks)
    def _(k):
        gather_copy(k).wait()

    full = lfull[...].reshape(rank, rows + LANES)
    inner_scores = full[:, :rows]
    group_scores = full[:, rows:]
    score_parts = jnp.concatenate(split(inner_scores), axis=0)
    part = stacked_dot(score_parts, rank, [parts[i] for i in range(3)], True)
    for i in range(tiles):
        between = group_scores * (float(rows) * apart[i : i + 1, :])
        spack[pl.ds(i, rank, stride=tiles), :] = part[:, i * LANES : (i + 1) * LANES] + between

    @pl.loop(1, curves)
    def _(k):
        sketch_copy(k).start()

    sparts[cg] = spack[pl.ds(pl.multiple_of(cg * owned, owned), owned), :]

    @pl.loop(1, blocks)
    def _(k):
        shift_copy(k).wait()

    shift = jnp.sum(uparts[...], axis=0)
    shift_col = jnp.transpose(jnp.broadcast_to(shift[0:1, :], (LANES, LANES)))[:rank, :1]
    score_ref[...] = inner_scores + shift_col

    @pl.loop(1, curves)
    def _(k):
        sketch_copy(k).wait()

    total = jnp.sum(sparts[...], axis=0) / (rows * curves)
    for p in range(rank // curves):
        for i in range(tiles):
            at = pl.ds(i * LANES, LANES)
            source = p * tiles + i
            sketch_ref[p : p + 1, at] = prevbuf[p : p + 1, at] + total[source : source + 1, :]


def finish(*refs):
    sources, results, sems = refs[:3], refs[3:6], refs[6]
    copies = [
        pltpu.make_async_copy(source, result, sems.at[i])
        for i, (source, result) in enumerate(zip(sources, results))
    ]
    for copy in copies:
        copy.start()
    for copy in copies:
        copy.wait()


def body(curves, blocks, samples, smoothing, test_matrix, sketch_prev):
    rows, taken = samples.shape
    width = taken // SPB
    rank = test_matrix.shape[1]
    halves = rows // LANES
    tiles = width // LANES
    chunks = taken // CHUNK
    share = rank // blocks
    owned = rank // curves * tiles
    f32 = jnp.float32
    vmem = pl.BlockSpec(memory_space=pltpu.VMEM)
    hbm = pl.BlockSpec(memory_space=pltpu.HBM)
    dma = pltpu.SemaphoreType.DMA
    tall = pltpu.VMEM((halves, width + 4 * TILE, LANES), f32)
    coef, score_t, sketch_t = pl.pallas_call(
        functools.partial(kernel, curves, blocks),
        out_shape=(
            jax.ShapeDtypeStruct((rows, width), f32),
            jax.ShapeDtypeStruct((rank, rows), f32),
            jax.ShapeDtypeStruct((rank // curves, width), f32),
        ),
        in_specs=[hbm] * 5,
        out_specs=(vmem, vmem, vmem),
        scratch_shapes=[
            pltpu.VMEM((chunks, rows, CHUNK), f32),
            pltpu.VMEM((2 * SPAN, CHUNK), jnp.bfloat16),
            pltpu.VMEM((halves, LANES), f32),
            pltpu.VMEM((rank, width), f32),
            pltpu.VMEM((rank // curves, width), f32),
            pltpu.VMEM((chunks, halves, SPAN, LANES), f32),
            pltpu.VMEM((halves, 2 * MARGIN, LANES), f32),
            pltpu.VMEM((halves, MARGIN, LANES), f32),
            tall,
            tall,
            tall,
            pltpu.VMEM((3, width, rows), jnp.bfloat16),
            pltpu.VMEM((TILE, LANES), f32),
            pltpu.VMEM((curves, TILE, LANES), f32),
            pltpu.VMEM((blocks, share, rows), f32),
            pltpu.VMEM((blocks, share, rows), f32),
            pltpu.VMEM((blocks, share, rows + LANES), f32),
            pltpu.VMEM((TILE, LANES), f32),
            pltpu.VMEM((blocks, TILE, LANES), f32),
            pltpu.VMEM((rank * tiles, LANES), f32),
            pltpu.VMEM((curves, owned, LANES), f32),
            dma((chunks,)),
            dma((4,)),
            dma((2,)),
            dma((2,)),
            dma((curves,)),
            dma((curves,)),
            dma((blocks,)),
            dma((blocks,)),
            dma((blocks,)),
            dma((blocks,)),
            dma((blocks,)),
            dma((blocks,)),
            dma((curves,)),
            dma((curves,)),
        ],
        compiler_params=pltpu.CompilerParams(
            collective_id=0, has_side_effects=True, vmem_limit_bytes=48 * 1024 * 1024
        ),
    )(
        *(
            pltpu.with_memory_space_constraint(value, pltpu.HBM)
            for value in (
                samples,
                smoothing.reshape(halves, LANES),
                test_matrix.T,
                sketch_prev.T,
                jnp.asarray(banded_table()),
            )
        )
    )
    coef, score_t, sketch_t = pl.pallas_call(
        finish,
        out_shape=(
            jax.ShapeDtypeStruct((rows, width), f32),
            jax.ShapeDtypeStruct((rank, rows), f32),
            jax.ShapeDtypeStruct((rank // curves, width), f32),
        ),
        in_specs=[vmem] * 3,
        out_specs=[hbm] * 3,
        scratch_shapes=[dma((3,))],
        compiler_params=pltpu.CompilerParams(vmem_limit_bytes=1048576),
    )(coef, score_t, sketch_t)
    return coef, score_t.T, sketch_t.T


def solution(mesh):
    placed = (P("curve", "tm"), P("curve"), P("tm", None), P("tm", "curve"))
    return jax.shard_map(
        functools.partial(body, mesh.shape["curve"], mesh.shape["tm"]),
        mesh=mesh,
        in_specs=placed,
        out_specs=(P("curve", "tm"), P("curve", None), P("tm", "curve")),
        check_vma=False,
    )
```

time: 47.2 us -> 36 us (0.76)
  Pallas kernels: 41.1 us -> 35.3 us
  local copies, waits for them, and re-layouts: 5.32 us -> 0 us
    pallas_call x1, Pallas kernels: 41.1 us -> 34.5 us  [body(): pl.pallas_call(functools.partial(kernel, curves, blocks), out_shape=(jax....]
    unnamed x11 -> x0, local copies, waits for them, and re-layouts: 5.32 us -> none
    pallas_call x0 -> x1, Pallas kernels: none -> 0.83 us  [body(): pl.pallas_call(finish, out_shape=(jax.ShapeDtypeStruct((rows, width), f32...]
where the time goes in v2:
time: 36 us; the launch traced here: 35.9 us
  Pallas kernels  35.3 us (98%)
  between operations  0.64 us (2%)
    pallas_call x1, Pallas kernels, body(): pl.pallas_call(functools.partial(kernel, curves, blocks), out_shape=(jax....  34.5 us
    pallas_call x1, Pallas kernels, body(): pl.pallas_call(finish, out_shape=(jax.ShapeDtypeStruct((rows, width), f32...  0.83 us

profile of v2, /device:TPU:1, one launch (start us, length us, event | category | flops | bytes accessed | tf_op | source)
XLA Modules:
  0.0 35.9 jit_solution(5644834033727899737)
XLA Ops:
  0.6 34.5 %shard_map.76 = (f32[256,512]{1,0:T(8,128)S(1)}, f32[64,256]{1,0:T(8,128)S(1)}, f32[2,512]{1,0:T(2,128)S(1)}) custom-call(f32[256,8192]{1,0:T(8,128)} %x_hbm.1, f32[2,128]{1,0:T(2,128)} %bitcast.7, f32[64,512]{1,0:T(8,128)} %bitcast.5, f32[2,512]{1,0:T(2,128)} %bitcast.6, bf16[144,1024]{1,0:T(8,128)(2,1)} %constant.2.clone.w_hbm), custom_call_target="tpu_custom_call" | custom-call | tf_op jit(solution)/shard_map/pallas_call | solution.py:472
  35.1 0.8 %shard_map.77 = (f32[256,512]{1,0:T(8,128)}, f32[64,256]{1,0:T(8,128)}, f32[2,512]{1,0:T(2,128)}) custom-call(f32[256,512]{1,0:T(8,128)S(1)} %get-tuple-element.9.refs_0_, f32[64,256]{1,0:T(8,128)S(1)} %get-tuple-element.10.refs_1_, f32[2,512]{1,0:T(2,128)S(1)} %get-tuple-element.11.refs_2_), custom_call_target="tpu_custom_call" | custom-call | tf_op jit(solution)/shard_map/pallas_call | solution.py:533

commit v3 on v2

--- a/solution.py
+++ b/solution.py
@@ -61,6 +61,21 @@
             piece = out[i * count : (i + 1) * count]
             total = piece if total is None else total + piece
     return total
+
+
+def far_first(curves, act):
+    quarter = curves // 4
+    act(3 * quarter)
+    act(quarter)
+
+    @pl.loop(1, quarter)
+    def _(d):
+        act(3 * quarter + d)
+        act(3 * quarter - d)
+        act(quarter + d)
+        act(quarter - d)
+
+    act(2 * quarter)
 
 
 def kernel(
@@ -139,16 +154,17 @@
 
     barrier = pltpu.get_barrier_semaphore()
 
+    def greet(k):
+        pl.semaphore_signal(
+            barrier, inc=1, device_id={"curve": lax.rem(cg + k, curves)}, device_id_type=MESH
+        )
+
+    far_first(curves, greet)
+
     @pl.loop(1, blocks)
     def _(k):
         pl.semaphore_signal(
             barrier, inc=1, device_id={"tm": lax.rem(tb + k, blocks)}, device_id_type=MESH
-        )
-
-    @pl.loop(1, curves)
-    def _(k):
-        pl.semaphore_signal(
-            barrier, inc=1, device_id={"curve": lax.rem(cg + k, curves)}, device_id_type=MESH
         )
 
     def project(c):
@@ -276,6 +292,16 @@
         at = pl.ds(h * LANES, LANES)
         for i, part in enumerate(split(even[h, pl.ds(own, width), :])):
             parts[i, :, at] = part
+    lane = lax.broadcasted_iota(jnp.int32, (LANES, LANES), 1)
+    line = lax.broadcasted_iota(jnp.int32, (LANES, LANES), 0)
+    for i in range(tiles):
+        at = pl.ds(own + i * LANES, LANES)
+        block = even[0, at, :]
+        for h in range(1, halves):
+            block += even[h, at, :]
+        mean = jnp.sum(block, axis=1, keepdims=True) / rows
+        msend[i : i + 1, :] = jnp.sum(jnp.where(lane == line, mean, 0.0), axis=0, keepdims=True)
+
     tt = ttbuf[...]
     tt_parts = jnp.concatenate(split(tt), axis=0)
     partial = stacked_dot(tt_parts, rank, [parts[i] for i in range(3)], False)
@@ -322,38 +348,46 @@
             device_id_type=MESH,
         )
 
-    def sketch_copy(k):
-        to = lax.rem(cg + k, curves)
+    def sketch_copy(source, to):
         return pltpu.make_async_remote_copy(
             src_ref=spack.at[pl.ds(pl.multiple_of(to * owned, owned), owned), :],
-            dst_ref=sparts.at[cg],
-            send_sem=f_send.at[k],
-            recv_sem=f_recv.at[k],
+            dst_ref=sparts.at[source],
+            send_sem=f_send.at[to],
+            recv_sem=f_recv.at[source],
             device_id={"curve": to},
             device_id_type=MESH,
         )
 
+    def sketch_of(chunks_at, scores):
+        count = len(chunks_at) * share
+        stacked = jnp.concatenate([p.astype(jnp.float32) for p in split(scores)], axis=0)
+        stacked = stacked.astype(jnp.bfloat16)
+        total = None
+        for used, i in ((3, 0), (2, 1), (1, 2)):
+            out = lax.dot_general(
+                stacked, parts[i], CONTRACT_LAST, preferred_element_type=jnp.float32
+            )
+            for n in range(used):
+                piece = out[n * count : (n + 1) * count]
+                total = piece if total is None else total + piece
+        for n, chunk in enumerate(chunks_at):
+            for i in range(tiles):
+                at = pl.ds(chunk * (share * tiles) + i, share, stride=tiles)
+                spack[at, :] = total[n * share : (n + 1) * share, i * LANES : (i + 1) * LANES]
+        for chunk in chunks_at:
+            for n in range(curves // blocks):
+                to = chunk * (curves // blocks) + n
+
+                @pl.when(to != cg)
+                def _(to=to):
+                    sketch_copy(cg, to).start()
+
     @pl.loop(1, blocks)
     def _(k):
         scatter_copy(k).start()
 
+    far_first(curves, lambda k: mean_copy(k).start())
     lparts[tb] = lsend[tb]
-
-    lane = lax.broadcasted_iota(jnp.int32, (LANES, LANES), 1)
-    line = lax.broadcasted_iota(jnp.int32, (LANES, LANES), 0)
-    msend[...] = jnp.zeros_like(msend)
-    for i in range(tiles):
-        at = pl.ds(own + i * LANES, LANES)
-        block = even[0, at, :]
-        for h in range(1, halves):
-            block += even[h, at, :]
-        mean = jnp.sum(block, axis=1, keepdims=True) / rows
-        msend[i : i + 1, :] = jnp.sum(jnp.where(lane == line, mean, 0.0), axis=0, keepdims=True)
-
-    @pl.loop(1, curves)
-    def _(k):
-        mean_copy(k).start()
-
     mall[cg] = msend[...]
 
     for h in range(halves):
@@ -366,81 +400,78 @@
         scatter_copy(k).wait()
 
     mine = jnp.sum(lparts[...], axis=0)
-    group_score = jnp.sum(mine, axis=1, keepdims=True) / rows
-    mine = mine - group_score
-    slip = jnp.sum(mine, axis=1, keepdims=True) / rows
-    lfull[tb] = jnp.concatenate(
-        [mine - slip, jnp.broadcast_to(group_score + slip, (share, LANES))], axis=1
+    mine = mine - jnp.sum(mine, axis=1, keepdims=True) / rows
+    mine = mine - jnp.sum(mine, axis=1, keepdims=True) / rows
+    lfull[tb] = mine
+
+    @pl.loop(1, blocks)
+    def _(k):
+        gather_copy(k).start()
+
+    sketch_of([tb], mine)
+    near_first = [[4, 1, 7], [3, 5], [2, 6]] if blocks == 8 else [list(range(1, blocks))]
+    for distances in near_first:
+        for k in distances:
+            gather_copy(blocks - k).wait_recv()
+        chunks_at = [lax.rem(tb + k, blocks) for k in distances]
+        sketch_of(chunks_at, jnp.concatenate([lfull[c] for c in chunks_at], axis=0))
+    sparts[cg] = spack[pl.ds(pl.multiple_of(cg * owned, owned), owned), :]
+
+    @pl.loop(1, curves)
+    def _(k):
+        mean_copy(k).wait()
+
+    apart = []
+    for i in range(tiles):
+        about = mall[:, i, :]
+        about = about - jnp.sum(about, axis=0, keepdims=True) / curves
+        apart.append(about - jnp.sum(about, axis=0, keepdims=True) / curves)
+    exact = dict(precision=lax.Precision.HIGHEST, preferred_element_type=jnp.float32)
+    shifts = lax.dot_general(jnp.concatenate(apart, axis=1), tt, CONTRACT_LAST, **exact)
+    group_at = lax.broadcasted_iota(jnp.int32, (curves, rank), 0)
+    per_owner = rank // curves
+    picks = usend.shape[1]
+    column = lax.broadcasted_iota(jnp.int32, (picks, rank), 1)
+    pick = lax.broadcasted_iota(jnp.int32, (picks, rank), 0)
+    chosen = (column == cg * per_owner + pick) & (pick < per_owner)
+    usend[...] = jnp.zeros_like(usend)
+    usend[0, :, pl.ds(0, rank)] = jnp.broadcast_to(
+        jnp.sum(jnp.where(group_at == cg, shifts, 0.0), axis=0, keepdims=True), (picks, rank)
     )
+    usend[1, :, pl.ds(0, curves)] = lax.dot_general(
+        chosen.astype(jnp.float32), shifts, CONTRACT_LAST, **exact
+    )
 
     @pl.loop(1, blocks)
     def _(k):
-        gather_copy(k).start()
+        shift_copy(k).start()
+
+    uparts[tb] = usend[...]
+
+    @pl.loop(1, blocks)
+    def _(k):
+        shift_copy(k).wait()
+        gather_copy(k).wait_send()
+
+    shift = jnp.sum(uparts[...], axis=0)
+    shift_col = jnp.transpose(jnp.broadcast_to(shift[0, 0:1, :], (LANES, LANES)))[:rank, :1]
+    score_ref[...] = lfull[...].reshape(rank, rows) + shift_col
+    between = [
+        jnp.dot(shift[1, :, :curves], apart[i], **exact) / curves for i in range(tiles)
+    ]
 
     @pl.loop(1, curves)
     def _(k):
-        mean_copy(k).wait()
-
-    means = mall[...]
-    rough = jnp.sum(means, axis=0) / curves
-    slip = jnp.sum(means - rough[None], axis=0) / curves
-    apart = (msend[...] - rough) - slip
-    apart_row = jnp.concatenate(
-        [jnp.broadcast_to(apart[i : i + 1, :], (TILE, LANES)) for i in range(tiles)], axis=1
-    )
-    shift_part = lax.dot_general(
-        apart_row,
-        tt,
-        CONTRACT_LAST,
-        precision=lax.Precision.HIGHEST,
-        preferred_element_type=jnp.float32,
-    )
-    usend[...] = jnp.zeros_like(usend)
-    usend[:, pl.ds(0, rank)] = shift_part
-
-    @pl.loop(1, blocks)
-    def _(k):
-        shift_copy(k).start()
-
-    uparts[tb] = usend[...]
-
-    @pl.loop(1, blocks)
-    def _(k):
-        gather_copy(k).wait()
-
-    full = lfull[...].reshape(rank, rows + LANES)
-    inner_scores = full[:, :rows]
-    group_scores = full[:, rows:]
-    score_parts = jnp.concatenate(split(inner_scores), axis=0)
-    part = stacked_dot(score_parts, rank, [parts[i] for i in range(3)], True)
-    for i in range(tiles):
-        between = group_scores * (float(rows) * apart[i : i + 1, :])
-        spack[pl.ds(i, rank, stride=tiles), :] = part[:, i * LANES : (i + 1) * LANES] + between
-
-    @pl.loop(1, curves)
-    def _(k):
-        sketch_copy(k).start()
-
-    sparts[cg] = spack[pl.ds(pl.multiple_of(cg * owned, owned), owned), :]
-
-    @pl.loop(1, blocks)
-    def _(k):
-        shift_copy(k).wait()
-
-    shift = jnp.sum(uparts[...], axis=0)
-    shift_col = jnp.transpose(jnp.broadcast_to(shift[0:1, :], (LANES, LANES)))[:rank, :1]
-    score_ref[...] = inner_scores + shift_col
-
-    @pl.loop(1, curves)
-    def _(k):
-        sketch_copy(k).wait()
+        other = lax.rem(cg + k, curves)
+        sketch_copy(other, other).wait()
 
     total = jnp.sum(sparts[...], axis=0) / (rows * curves)
-    for p in range(rank // curves):
+    for p in range(per_owner):
         for i in range(tiles):
             at = pl.ds(i * LANES, LANES)
             source = p * tiles + i
-            sketch_ref[p : p + 1, at] = prevbuf[p : p + 1, at] + total[source : source + 1, :]
+            summed = total[source : source + 1, :] + between[i][p : p + 1, :]
+            sketch_ref[p : p + 1, at] = prevbuf[p : p + 1, at] + summed
 
 
 def finish(*refs):
@@ -464,6 +495,7 @@
     chunks = taken // CHUNK
     share = rank // blocks
     owned = rank // curves * tiles
+    picks = -(-(rank // curves) // TILE) * TILE
     f32 = jnp.float32
     vmem = pl.BlockSpec(memory_space=pltpu.VMEM)
     hbm = pl.BlockSpec(memory_space=pltpu.HBM)
@@ -491,13 +523,13 @@
             tall,
             tall,
             pltpu.VMEM((3, width, rows), jnp.bfloat16),
-            pltpu.VMEM((TILE, LANES), f32),
-            pltpu.VMEM((curves, TILE, LANES), f32),
+            pltpu.VMEM((tiles, LANES), f32),
+            pltpu.VMEM((curves, tiles, LANES), f32),
             pltpu.VMEM((blocks, share, rows), f32),
             pltpu.VMEM((blocks, share, rows), f32),
-            pltpu.VMEM((blocks, share, rows + LANES), f32),
-            pltpu.VMEM((TILE, LANES), f32),
-            pltpu.VMEM((blocks, TILE, LANES), f32),
+            pltpu.VMEM((blocks, share, rows), f32),
+            pltpu.VMEM((2, picks, LANES), f32),
+            pltpu.VMEM((blocks, 2, picks, LANES), f32),
             pltpu.VMEM((rank * tiles, LANES), f32),
             pltpu.VMEM((curves, owned, LANES), f32),
             dma((chunks,)),

time: 36 us -> 33.9 us (0.942)
  the two profiles are of different devices: /device:TPU:1 before, /device:TPU:7 now
where the time goes in v3:
time: 33.9 us; the launch traced here: 33.8 us
  Pallas kernels  33.2 us (98%)
  between operations  0.64 us (2%)
    pallas_call x1, Pallas kernels, body(): pl.pallas_call(functools.partial(kernel, curves, blocks), out_shape=(jax....  32.3 us
    pallas_call x1, Pallas kernels, body(): pl.pallas_call(finish, out_shape=(jax.ShapeDtypeStruct((rows, width), f32...  0.83 us

profile of v3, /device:TPU:7, one launch (start us, length us, event | category | flops | bytes accessed | tf_op | source)
XLA Modules:
  0.0 33.8 jit_solution(5382744287152080158)
XLA Ops:
  0.6 32.3 %shard_map.76 = (f32[256,512]{1,0:T(8,128)S(1)}, f32[64,256]{1,0:T(8,128)S(1)}, f32[2,512]{1,0:T(2,128)S(1)}) custom-call(f32[256,8192]{1,0:T(8,128)} %x_hbm.1, f32[2,128]{1,0:T(2,128)} %bitcast.7, f32[64,512]{1,0:T(8,128)} %bitcast.5, f32[2,512]{1,0:T(2,128)} %bitcast.6, bf16[144,1024]{1,0:T(8,128)(2,1)} %constant.2.clone.w_hbm), custom_call_target="tpu_custom_call" | custom-call | tf_op jit(solution)/shard_map/pallas_call | solution.py:504
  33.0 0.8 %shard_map.77 = (f32[256,512]{1,0:T(8,128)}, f32[64,256]{1,0:T(8,128)}, f32[2,512]{1,0:T(2,128)}) custom-call(f32[256,512]{1,0:T(8,128)S(1)} %get-tuple-element.9.refs_0_, f32[64,256]{1,0:T(8,128)S(1)} %get-tuple-element.10.refs_1_, f32[2,512]{1,0:T(2,128)S(1)} %get-tuple-element.11.refs_2_), custom_call_target="tpu_custom_call" | custom-call | tf_op jit(solution)/shard_map/pallas_call | solution.py:565
